TPU v7x, 32 devices: a whole 2x2x4 slice. The times are simulated.
32 devices in a mesh: grp: 2 (over y), sv: 4 (over z), tv: 4 (over x, core).
Axes of the slice: x: 2, y: 2, z: 4, core: 2. Of those that a mesh axis runs over, the one named last changes fastest.
Arguments:
- student_states: bfloat16 [512, 1792], P('grp', 'tv'), parts along dimension 0, may hold values from -60 to 60
- teacher_states: bfloat16 [512, 2304], P('grp', 'tv'), parts along dimension 0, may hold values from -60 to 60
- student_queries: bfloat16 [512, 256], P('grp', 'tv'), parts along dimension 0, may hold values from -60 to 60
- teacher_keys: bfloat16 [512, 256], P('grp', 'tv'), parts along dimension 0, may hold values from -6 to 6
- student_targets: int32 [512], P('grp'), parts along dimension 0, may hold values from 0 to 8191
- teacher_targets: int32 [512], P('grp'), parts along dimension 0, may hold values from 0 to 8191
- student_lengths: int32 [4], P('grp'), parts along dimension 0, may hold values from 64 to 128
- teacher_lengths: int32 [4], P('grp'), parts along dimension 0, may hold values from 64 to 128
- to_teacher: bfloat16 [1792, 2304], P('tv', 'sv'), may hold values from -0.125 to 0.125
- to_student: bfloat16 [2304, 1792], P('tv', 'sv'), may hold values from -0.125 to 0.125
- student_head: bfloat16 [1792, 8192], P(None, ('sv', 'tv')), may hold values from -0.125 to 0.125
- teacher_head: bfloat16 [2304, 8192], P(None, ('sv', 'tv')), may hold values from -0.125 to 0.125
Outputs:
- student_loss: float32 [512], P('grp'), parts along dimension 0
- teacher_loss: float32 [512], P('grp'), parts along dimension 0
- student_grad: bfloat16 [512, 8192], P('grp', ('sv', 'tv')), parts along dimension 0
- teacher_grad: bfloat16 [512, 8192], P('grp', ('sv', 'tv')), parts along dimension 0
There are 2 independent parts, one for each index of `grp`. A program takes and returns all parts, laid end to end along the dimension named above; an argument that names none is the same for every part. Nothing has to cross between parts.
All inputs are finite; a program needn't handle non-finite values.
Results may differ from a plain program's by a relative error of at most 0.0086.
Values may be sent and summed in bfloat16 or wider, within the bound.
No kernel may reach another device: no remote copies, remote signals or barrier semaphores. Data moves between devices by JAX's collectives and lax.ppermute only.
A program may use at most 64 MiB of HBM per device.

v0:
```python
import jax
import jax.numpy as jnp
from jax import lax
from jax.sharding import PartitionSpec as P

DK = 256
floor_value = -1e30


def combined_all(part, axis, combine):
    gathered = jax.tree.map(lambda a: lax.all_gather(a, axis), part)

    def take(source):
        return jax.tree.map(lambda a: lax.dynamic_index_in_dim(a, source, 0, False), gathered)

    return lax.fori_loop(
        1, lax.axis_size(axis), lambda source, state: combine(state, take(source)), take(0)
    )


def align_block(student_queries, teacher_keys, teacher_states, teacher_lengths):
    sequences = teacher_lengths.shape[0]
    query_cols = student_queries.shape[1]
    queries = student_queries.reshape(sequences, -1, query_cols)
    keyset = teacher_keys.reshape(sequences, -1, query_cols)
    partial_scores = jnp.einsum("sid,sjd->sij", queries, keyset, preferred_element_type=jnp.float32)
    scores = lax.psum(partial_scores, "tv") * DK ** (-0.5)
    positions = lax.broadcasted_iota(jnp.int32, scores.shape, 2)
    scores = jnp.where(positions < teacher_lengths[:, None, None], scores, floor_value)
    highest = jnp.max(scores, axis=2, keepdims=True)
    weights = jnp.exp(scores - highest)
    weights = (weights / jnp.sum(weights, axis=2, keepdims=True)).astype(jnp.bfloat16)
    states = teacher_states.reshape(sequences, -1, teacher_states.shape[1])
    aligned = jnp.einsum("sij,sjd->sid", weights, states, preferred_element_type=jnp.float32)
    return aligned.astype(jnp.bfloat16).reshape(-1, teacher_states.shape[1])


def live_rows(row_count, lengths, sequence_length):
    indices = lax.broadcasted_iota(jnp.int32, (row_count,), 0)
    sequence = indices // sequence_length
    position = indices % sequence_length
    owners = lax.broadcasted_iota(jnp.int32, (row_count, lengths.shape[0]), 1)
    length_limit = jnp.sum(jnp.where(sequence[:, None] == owners, lengths[None, :], 0), axis=1)
    return (position < length_limit).astype(jnp.float32)


def local_stats(logits, target_cols, kind_index):
    other_kind = 1 - kind_index
    highest = jnp.max(logits, axis=2)
    scaled = jnp.exp(logits - highest[:, :, None])
    totals = jnp.sum(scaled, axis=2)
    spread = jnp.sum(
        scaled[:, kind_index] * (logits[:, kind_index] - logits[:, other_kind]), axis=1
    )
    column = lax.broadcasted_iota(jnp.int32, logits.shape, 2)
    picked = jnp.sum(jnp.where(column == target_cols[:, None, None], logits, 0.0), axis=2)
    return (highest, totals, spread, picked)


def side_combine(former, latter, kind_index):
    highest = jnp.maximum(former[0], latter[0])
    former_scale = jnp.exp(former[0] - highest)
    latter_scale = jnp.exp(latter[0] - highest)
    totals = former[1] * former_scale + latter[1] * latter_scale
    spread = former[2] * former_scale[:, kind_index] + latter[2] * latter_scale[:, kind_index]
    return (highest, totals, spread, former[3] + latter[3])


def student_combine(former, latter):
    return side_combine(former, latter, 1)


def teacher_combine(former, latter):
    return side_combine(former, latter, 0)


def side_terms(logits, statistics, target_cols):
    highest, totals = (statistics[0], statistics[1])
    log_total = highest + jnp.log(totals)
    chances = jnp.exp(logits - log_total[:, :, None])
    column = lax.broadcasted_iota(jnp.int32, chances[:, 0].shape, 1)
    target_hot = (column == target_cols[:, None]).astype(jnp.float32)
    return (log_total, chances, target_hot)


def student_side(logits, statistics, target_cols, live_mask):
    log_total, chances, target_hot = side_terms(logits, statistics, target_cols)
    totals, spread, picked = (statistics[1], statistics[2], statistics[3])
    diverge = spread / totals[:, 1] - log_total[:, 1] + log_total[:, 0]
    row_loss = live_mask * (
        log_total[:, 0] - picked[:, 0] + log_total[:, 1] - picked[:, 1] + diverge
    )
    gradient = live_mask[:, None] * (2.0 * chances[:, 0] - target_hot - chances[:, 1])
    return (row_loss, gradient.astype(jnp.bfloat16))


def teacher_side(logits, statistics, target_cols, live_mask):
    log_total, chances, target_hot = side_terms(logits, statistics, target_cols)
    totals, spread, picked = (statistics[1], statistics[2], statistics[3])
    diverge = spread / totals[:, 0] - log_total[:, 0] + log_total[:, 1]
    row_loss = live_mask * (diverge + log_total[:, 1] - picked[:, 1])
    gradient = live_mask[:, None] * (2.0 * chances[:, 1] - chances[:, 0] - target_hot)
    return (row_loss, gradient.astype(jnp.bfloat16))


def body(
    student_states,
    teacher_states,
    student_queries,
    teacher_keys,
    student_targets,
    teacher_targets,
    student_lengths,
    teacher_lengths,
    to_teacher,
    to_student,
    student_head,
    teacher_head,
):
    row_total = student_states.shape[0]
    sequence_length = row_total // student_lengths.shape[0]
    sv_index = lax.axis_index("sv")
    tv_index = lax.axis_index("tv")
    tv_count = lax.axis_size("tv")
    vocab_block = sv_index * tv_count + tv_index
    aligned_block = align_block(student_queries, teacher_keys, teacher_states, teacher_lengths)
    full_student = lax.all_gather(student_states, "tv", axis=1, tiled=True)
    full_aligned = lax.all_gather(aligned_block, "tv", axis=1, tiled=True)
    teacher_part = lax.psum(
        jnp.dot(student_states, to_teacher, preferred_element_type=jnp.float32), "tv"
    )
    student_part = lax.psum(
        jnp.dot(aligned_block, to_student, preferred_element_type=jnp.float32), "tv"
    )
    into_teacher = lax.all_gather(teacher_part.astype(jnp.bfloat16), "sv", axis=1, tiled=True)
    into_student = lax.all_gather(student_part.astype(jnp.bfloat16), "sv", axis=1, tiled=True)
    student_logits = jnp.stack(
        [
            jnp.dot(full_student, student_head, preferred_element_type=jnp.float32),
            jnp.dot(into_student, student_head, preferred_element_type=jnp.float32),
        ],
        axis=1,
    )
    student_cols = student_targets - vocab_block * student_head.shape[1]
    student_stats = local_stats(student_logits, student_cols, 1)
    teacher_logits = jnp.stack(
        [
            jnp.dot(full_aligned, teacher_head, preferred_element_type=jnp.float32),
            jnp.dot(into_teacher, teacher_head, preferred_element_type=jnp.float32),
        ],
        axis=1,
    )
    teacher_cols = teacher_targets - vocab_block * teacher_head.shape[1]
    teacher_stats = local_stats(teacher_logits, teacher_cols, 0)
    student_stats = combined_all(student_stats, ("sv", "tv"), student_combine)
    teacher_stats = combined_all(teacher_stats, ("sv", "tv"), teacher_combine)
    every_live = live_rows(row_total, student_lengths, sequence_length)
    student_loss, student_grad = student_side(
        student_logits, student_stats, student_cols, every_live
    )
    teacher_loss, teacher_grad = teacher_side(
        teacher_logits, teacher_stats, teacher_cols, every_live
    )
    return (student_loss, teacher_loss, student_grad, teacher_grad)


def solution(mesh):
    in_specs = (
        P("grp", "tv"),
        P("grp", "tv"),
        P("grp", "tv"),
        P("grp", "tv"),
        P("grp"),
        P("grp"),
        P("grp"),
        P("grp"),
        P("tv", "sv"),
        P("tv", "sv"),
        P(None, ("sv", "tv")),
        P(None, ("sv", "tv")),
    )
    out_specs = (P("grp"), P("grp"), P("grp", ("sv", "tv")), P("grp", ("sv", "tv")))
    return jax.shard_map(body, mesh=mesh, in_specs=in_specs, out_specs=out_specs, check_vma=False)
```

profile of v0, /device:TPU:0, one launch (start us, length us, event | category | flops | bytes accessed | tf_op | source)
XLA Modules:
  0.0 294.7 jit_solution(5090712872728876629)
XLA Ops:
  7.2 0.0 copy-start
  7.2 0.0 copy-start.5
  7.2 0.0 copy-start.15
  7.2 0.0 copy-start.16
  7.2 0.0 copy-start.17
  7.2 0.0 all-reduce.4.cloned.1.call-start
  7.3 1.8 fusion.30
  9.1 0.0 all-reduce.4.cloned.1.call-update
  9.1 0.0 all-gather.15.cloned.1.call-start
  9.2 12.4 %all_gather.60 = bf16[256,1792]{0,1:T(8,128)(2,1)} all-gather(bf16[256,448]{0,1:T(8,128)(2,1)} %param.16), channel_id=1, replica_groups=mesh['grp'=2,'sv'=4,'tv'=4] {'tv'}, dimensions={1}, use_global_device_ids=true | all-gather | bytes 1146880 | tf_op jit(solution)/shard_map/all_gather | solution.py:127
  21.6 1.3 fusion.60
  22.9 0.0 copy-done.15
  22.9 0.0 copy-done.16
  22.9 0.0 copy-done.17
  23.0 0.1 fusion.35
  23.0 22.0 %all-reduce.4.cloned.1.call-done = f32[2,128,128]{2,1,0:T(8,128)} async-done(((f32[2,128,128]{2,1,0:T(8,128)}), f32[2,128,128]{2,1,0:T(8,128)}) %all-reduce.4.cloned.1.call-update) | async-done | bytes 131088 | tf_op jit(solution)/shard_map/psum | solution.py:27
  45.1 1.2 fusion.56
  46.3 2.4 fusion.5
  48.7 1.5 fusion.48
  50.1 26.0 %all-reduce.5 = (bf16[256,448]{0,1:T(8,128)(2,1)}, bf16[256,576]{0,1:T(8,128)(2,1)}) all-reduce(f32[256,448]{0,1:T(8,128)S(1)} %fusion.48, f32[256,576]{0,1:T(8,128)S(1)} %fusion.60), channel_id=1, replica_groups=mesh['grp'=2,'sv'=4,'tv'=4] {'tv'}, use_global_device_ids=true, to_apply=%region_4.5 | all-reduce | flops 262144 | bytes 1572864 | tf_op jit(solution)/shard_map/psum | solution.py:132
  76.2 0.0 all-gather.15.cloned.1.call-update
  76.2 0.0 all-gather.13.cloned.1.call-start
  76.2 0.6 fusion.47
  76.8 2.6 fusion.57
  79.4 0.8 copy.53
  80.2 33.6 %all_gather.61 = bf16[256,1792]{0,1:T(8,128)(2,1)S(1)} all-gather(bf16[256,448]{0,1:T(8,128)(2,1)S(1)} %copy-done.6), channel_id=1, replica_groups=mesh['grp'=2,'sv'=4,'tv'=4] {'sv'}, dimensions={1}, use_global_device_ids=true | all-gather | bytes 1146880 | tf_op jit(solution)/shard_map/all_gather | solution.py:136
  113.8 0.7 fusion.58
  114.5 0.4 select_reduce_fusion.1
  114.8 0.3 fusion.52
  115.1 0.2 fusion.20
  115.3 20.8 %all-gather.8 = f32[16,1,256]{2,1,0:T(1,128)S(1)} all-gather(f32[1,1,256]{2,1,0:T(1,128)S(1)} %bitcast.187), channel_id=4, replica_groups=mesh['grp'=2,'sv'=4,'tv'=4] {'sv','tv'}, dimensions={0}, use_global_device_ids=true | all-gather | bytes 17408 | tf_op jit(solution)/shard_map/all_gather | solution.py:11
  136.1 17.5 %all-gather = f32[4096,2]{0,1:T(2,128)S(1)} all-gather(f32[256,2]{0,1:T(2,128)S(1)} %get-tuple-element.461), channel_id=2, replica_groups=mesh['grp'=2,'sv'=4,'tv'=4] {'sv','tv'}, dimensions={0}, use_global_device_ids=true | all-gather | bytes 34816 | tf_op jit(solution)/shard_map/all_gather | solution.py:11
  153.6 18.9 %all-gather.1 = f32[4096,2]{0,1:T(2,128)S(1)} all-gather(f32[256,2]{0,1:T(2,128)S(1)} %get-tuple-element.510), channel_id=3, replica_groups=mesh['grp'=2,'sv'=4,'tv'=4] {'sv','tv'}, dimensions={0}, use_global_device_ids=true | all-gather | bytes 34816 | tf_op jit(solution)/shard_map/all_gather | solution.py:11
  172.4 17.5 %all-gather.3 = f32[4096,2]{0,1:T(2,128)S(1)} all-gather(f32[256,2]{0,1:T(2,128)S(1)} %get-tuple-element.460), channel_id=5, replica_groups=mesh['grp'=2,'sv'=4,'tv'=4] {'sv','tv'}, dimensions={0}, use_global_device_ids=true | all-gather | bytes 34816 | tf_op jit(solution)/shard_map/all_gather | solution.py:11
  189.9 0.0 all-gather.13.cloned.1.call-update
  189.9 1.6 while.42
  191.5 0.6 slice.101
  192.1 0.6 fusion.55
  192.7 0.6 fusion.54
  193.3 2.9 fusion.61
  196.2 9.7 %all-gather.13.cloned.1.call-done = bf16[256,2304]{0,1:T(8,128)(2,1)} async-done(((bf16[256,576]{0,1:T(8,128)(2,1)}), bf16[256,2304]{0,1:T(8,128)(2,1)}) %all-gather.13.cloned.1.call-update) | async-done | bytes 1179664 | tf_op jit(solution)/shard_map/all_gather | solution.py:128
  205.9 2.1 fusion.59
  208.0 0.0 copy-start.2
  208.1 0.0 copy-done.1
  208.1 0.4 select_reduce_fusion
  208.4 20.5 %all-gather.4 = f32[4096,2]{0,1:T(2,128)S(1)} all-gather(f32[256,2]{0,1:T(2,128)S(1)} %get-tuple-element.459), channel_id=6, replica_groups=mesh['grp'=2,'sv'=4,'tv'=4] {'sv','tv'}, dimensions={0}, use_global_device_ids=true | all-gather | bytes 34816 | tf_op jit(solution)/shard_map/all_gather | solution.py:11
  228.9 0.3 fusion.51
  229.2 0.2 fusion.18
  229.4 0.0 copy-done.2
  229.4 17.4 %all-gather.9 = f32[16,1,256]{2,1,0:T(1,128)S(1)} all-gather(f32[1,1,256]{2,1,0:T(1,128)S(1)} %bitcast.188), channel_id=8, replica_groups=mesh['grp'=2,'sv'=4,'tv'=4] {'sv','tv'}, dimensions={0}, use_global_device_ids=true | all-gather | bytes 17408 | tf_op jit(solution)/shard_map/all_gather | solution.py:11
  246.8 18.8 %all-gather.5 = f32[4096,2]{0,1:T(2,128)S(1)} all-gather(f32[256,2]{0,1:T(2,128)S(1)} %get-tuple-element.508), channel_id=7, replica_groups=mesh['grp'=2,'sv'=4,'tv'=4] {'sv','tv'}, dimensions={0}, use_global_device_ids=true | all-gather | bytes 34816 | tf_op jit(solution)/shard_map/all_gather | solution.py:11
  265.7 17.5 %all-gather.7 = f32[4096,2]{0,1:T(2,128)S(1)} all-gather(f32[256,2]{0,1:T(2,128)S(1)} %get-tuple-element.458), channel_id=9, replica_groups=mesh['grp'=2,'sv'=4,'tv'=4] {'sv','tv'}, dimensions={0}, use_global_device_ids=true | all-gather | bytes 34816 | tf_op jit(solution)/shard_map/all_gather | solution.py:11
  283.2 1.6 while.43
  284.8 0.0 copy-start.9
  284.8 1.5 subtract_exponential_fusion.2
  286.4 0.0 copy-start.8
  286.4 0.0 copy-start.10
  286.4 0.0 copy-start.11
  286.4 1.1 fusion.11
  287.5 0.0 copy-done.11
  287.5 0.0 copy-done.12
  287.6 0.0 copy-done.13
  287.6 0.0 copy-done.14
  287.6 0.6 fusion.37
  (188 shorter events, 1.9 us)
Async XLA Ops:
  7.2 186.1 %copy-start = (bf16[2304,512]{1,0:T(8,128)(2,1)S(1)}, bf16[2304,512]{1,0:T(8,128)(2,1)}, u32[]{:S(2)}) copy-start(bf16[2304,512]{1,0:T(8,128)(2,1)} %param.27) | copy-start | bytes 7077892
  7.2 14.4 %copy-start.5 = (bf16[448,576]{1,0:T(8,128)(2,1)S(1)}, bf16[448,576]{1,0:T(8,128)(2,1)}, u32[]{:S(2)}) copy-start(bf16[448,576]{1,0:T(8,128)(2,1)} %param.24) | copy-start | bytes 1548292
  7.2 15.7 %copy-start.15 = (s32[256]{0:T(256)S(1)}, s32[256]{0:T(256)}, u32[]{:S(2)}) copy-start(s32[256]{0:T(256)} %param.21) | copy-start | bytes 3076
  7.2 15.7 %copy-start.16 = (s32[256]{0:T(256)S(1)}, s32[256]{0:T(256)}, u32[]{:S(2)}) copy-start(s32[256]{0:T(256)} %param.20) | copy-start | bytes 3076
  7.2 15.7 %copy-start.17 = (s32[2]{0:T(128)S(1)}, s32[2]{0:T(128)}, u32[]{:S(2)}) copy-start(s32[2]{0:T(128)} %param.22) | copy-start | bytes 28
  7.2 37.9 %copy-start.18 = (s32[2]{0:T(128)S(1)}, s32[2]{0:T(128)}, u32[]{:S(2)}) copy-start(s32[2]{0:T(128)} %param.23) | copy-start | bytes 28
  7.2 37.9 %all-reduce.4.cloned.1.call-start = ((), (), s32[]{:S(2)}) async-start(), calls=%async_computation | async-start | bytes 262144 | tf_op jit(solution)/shard_map/psum | solution.py:27
  9.1 184.2 %all-gather.15.cloned.1.call-start = ((), (), s32[]{:S(2)}) async-start(), calls=%async_computation.2 | async-start | bytes 1474560 | tf_op jit(solution)/shard_map/all_gather | solution.py:135
  23.0 53.2 %copy-start.7 = (s32[256]{0:T(256)}, s32[256]{0:T(256)S(1)}, u32[]{:S(2)}) copy-start(s32[256]{0:T(256)S(1)} %fusion.35) | copy-start | bytes 3076
  76.2 3.2 %copy-start.4 = (bf16[2,72,8,128]{3,2,1,0:T(8,128)(2,1)S(1)}, bf16[2,72,8,128]{3,2,1,0:T(8,128)(2,1)}, u32[]{:S(2)}) copy-start(bf16[2,72,8,128]{3,2,1,0:T(8,128)(2,1)} %fusion.5) | copy-start | bytes 884740
  76.2 129.7 %all-gather.13.cloned.1.call-start = ((), (), s32[]{:S(2)}) async-start(), calls=%async_computation.1 | async-start | bytes 1474560 | tf_op jit(solution)/shard_map/all_gather | solution.py:128
  76.8 3.4 %copy-start.6 = (bf16[256,448]{0,1:T(8,128)(2,1)S(1)}, bf16[256,448]{0,1:T(8,128)(2,1)}, u32[]{:S(2)}) copy-start(bf16[256,448]{0,1:T(8,128)(2,1)} %get-tuple-element.498) | copy-start | bytes 688132
  76.8 37.0 %copy-start.3 = (bf16[1792,512]{1,0:T(8,128)(2,1)S(1)}, bf16[1792,512]{1,0:T(8,128)(2,1)}, u32[]{:S(2)}) copy-start(bf16[1792,512]{1,0:T(8,128)(2,1)} %param.26) | copy-start | bytes 5505028
  205.9 2.1 copy-start.1
  208.0 21.3 %copy-start.2 = (f32[256,512]{1,0:T(8,128)}, f32[256,512]{1,0:T(8,128)S(1)}, u32[]{:S(2)}) copy-start(f32[256,512]{1,0:T(8,128)S(1)} %fusion.59) | copy-start | bytes 1572868
  284.8 1.6 copy-start.9
  286.4 1.2 copy-start.8
  286.4 1.2 copy-start.10
  286.4 1.2 copy-start.11
  286.4 1.2 copy-start.12
  286.4 1.2 copy-start.13
  286.4 1.2 copy-start.14
Sparse Core Ops, SparseCore 0:
  11.0 34.0 all-reduce.3
  76.3 43.0 all-gather.14
  190.0 15.8 all-gather.12
where the time goes:
time: 295 us
  blocking collectives  221 us (75%)
  waiting for transfers between devices  31.8 us (11%)
  matrix products  15.3 us (5%)
  between operations  14.1 us (5%)
  other arithmetic  8 us (3%)
  local copies, waits for them, and re-layouts  3.24 us (1%)
    all_gather x8, blocking collectives, combined_all(): gathered = jax.tree.map(lambda a: lax.all_gather(a, axis), part)  149 us
    all_gather x1, blocking collectives, body(): lax.all_gather(student_part.astype(jnp.bfloat16), 'sv', axis=1, tiled=True)  33.6 us
    psum x1, blocking collectives, body(): lax.psum(jnp.dot(aligned_block, to_student, preferred_element_type=jnp.fl...  26 us
    psum x1, waiting for transfers between devices, align_block(): scores = lax.psum(partial_scores, 'tv') * DK ** (-0.5)  22 us
    all_gather x1, blocking collectives, body(): full_student = lax.all_gather(student_states, 'tv', axis=1, tiled=True)  12.4 us
    all_gather x1, waiting for transfers between devices, body(): full_aligned = lax.all_gather(aligned_block, 'tv', axis=1, tiled=True)  9.69 us
  transfers between devices with their start and end apart: 3, of which 2 were waited for; matrix products, arithmetic and copies ran while one was open for 4% of the time, Pallas kernels for 0%

commit v1 on v0

--- a/solution.py
+++ b/solution.py
@@ -129,9 +129,9 @@
     teacher_part = lax.psum(
         jnp.dot(student_states, to_teacher, preferred_element_type=jnp.float32), "tv"
     )
-    student_part = lax.psum(
-        jnp.dot(aligned_block, to_student, preferred_element_type=jnp.float32), "tv"
-    )
+    own = jnp.dot(aligned_block, to_student, preferred_element_type=jnp.float32)
+    parts = lax.all_gather(own, "tv")
+    student_part = jnp.sum(parts, axis=0)
     into_teacher = lax.all_gather(teacher_part.astype(jnp.bfloat16), "sv", axis=1, tiled=True)
     into_student = lax.all_gather(student_part.astype(jnp.bfloat16), "sv", axis=1, tiled=True)
     student_logits = jnp.stack(

time: 295 us -> 276 us (0.936)
  blocking collectives: 221 us -> 195 us
    all_gather x1, blocking collectives: 33.6 us -> 19.8 us  [body(): lax.all_gather(student_part.astype(jnp.bfloat16), 'sv', axis=1, tiled=True)]
    psum x1, waiting for transfers between devices: 22 us -> 14.7 us  [align_block(): scores = lax.psum(partial_scores, 'tv') * DK ** (-0.5)]
    all_gather x1, waiting for transfers between devices: 9.69 us -> 16 us  [body(): full_aligned = lax.all_gather(aligned_block, 'tv', axis=1, tiled=True)]
    psum x1, blocking collectives: 26 us -> 19.8 us  [body(): lax.psum(jnp.dot(student_states, to_teacher, preferred_element_type=jnp.f...]
    all_gather x1, blocking collectives: 12.4 us -> 7.89 us  [body(): full_student = lax.all_gather(student_states, 'tv', axis=1, tiled=True)]
    all_gather x0 -> x1, local copies, waits for them, and re-layouts: none -> 2.97 us  [body(): parts = lax.all_gather(own, 'tv')]
  transfers between devices with their start and end apart: 3 -> 4, of which waited for: 2 -> 3; matrix products, arithmetic and copies ran while one was open for 4% -> 6% of each run, Pallas kernels for 0% -> 0%
where the time goes in v1:
time: 276 us; the launch traced here: 275 us
  blocking collectives  195 us (71%)
  waiting for transfers between devices  31.4 us (11%)
  between operations  16 us (6%)
  matrix products  14.6 us (5%)
  other arithmetic  10.6 us (4%)
  local copies, waits for them, and re-layouts  6.14 us (2%)
    all_gather x8, blocking collectives, combined_all(): gathered = jax.tree.map(lambda a: lax.all_gather(a, axis), part)  148 us
    psum x1, blocking collectives, body(): lax.psum(jnp.dot(student_states, to_teacher, preferred_element_type=jnp.f...  19.8 us
    all_gather x1, blocking collectives, body(): lax.all_gather(student_part.astype(jnp.bfloat16), 'sv', axis=1, tiled=True)  19.8 us
    all_gather x1, waiting for transfers between devices, body(): full_aligned = lax.all_gather(aligned_block, 'tv', axis=1, tiled=True)  16 us
    psum x1, waiting for transfers between devices, align_block(): scores = lax.psum(partial_scores, 'tv') * DK ** (-0.5)  14.7 us
    all_gather x1, blocking collectives, body(): full_student = lax.all_gather(student_states, 'tv', axis=1, tiled=True)  7.89 us
  transfers between devices with their start and end apart: 4, of which 3 were waited for; matrix products, arithmetic and copies ran while one was open for 6% of the time, Pallas kernels for 0%

profile of v1, /device:TPU:0, one launch (start us, length us, event | category | flops | bytes accessed | tf_op | source)
XLA Modules:
  0.0 275.5 jit_solution(11142467365225751039)
XLA Ops:
  8.0 0.0 copy-start
  8.0 0.0 copy-start.15
  8.0 0.0 all-reduce.3.cloned.1.call-start
  8.1 1.8 fusion.30
  9.9 0.0 all-reduce.3.cloned.1.call-update
  9.9 0.0 all-gather.17.cloned.1.call-start
  9.9 1.6 fusion.60
  11.5 0.0 copy-start.14
  11.5 0.0 copy-start.12
  11.5 0.0 copy-start.13
  11.6 0.0 copy-start.3
  11.6 19.8 %all-reduce.4 = bf16[256,576]{0,1:T(8,128)(2,1)} all-reduce(f32[256,576]{0,1:T(8,128)S(1)} %fusion.60), channel_id=1, replica_groups=mesh['grp'=2,'sv'=4,'tv'=4] {'tv'}, use_global_device_ids=true, to_apply=%region_11.12 | all-reduce | flops 147456 | bytes 884736 | tf_op jit(solution)/shard_map/psum | solution.py:129
  31.4 0.0 all-gather.17.cloned.1.call-update
  31.4 0.0 all-gather.15.cloned.1.call-start
  31.5 14.7 %all-reduce.3.cloned.1.call-done = f32[2,128,128]{2,1,0:T(8,128)} async-done(((f32[2,128,128]{2,1,0:T(8,128)}), f32[2,128,128]{2,1,0:T(8,128)}) %all-reduce.3.cloned.1.call-update) | async-done | bytes 131088 | tf_op jit(solution)/shard_map/psum | solution.py:27
  46.1 1.2 fusion.56
  47.3 1.7 fusion.5
  49.0 0.8 copy.53
  49.7 0.0 all-gather.15.cloned.1.call-update
  49.8 0.0 all-gather.19.cloned.1.call-start
  49.8 0.1 fusion.35
  49.9 0.0 copy-done.12
  50.0 0.6 fusion.47
  50.5 0.0 copy-done.3
  50.5 7.9 %all_gather.66 = bf16[256,1792]{0,1:T(8,128)(2,1)S(1)} all-gather(bf16[256,448]{0,1:T(8,128)(2,1)S(1)} %copy-done.3), channel_id=1, replica_groups=mesh['grp'=2,'sv'=4,'tv'=4] {'tv'}, dimensions={1}, use_global_device_ids=true | all-gather | bytes 1146880 | tf_op jit(solution)/shard_map/all_gather | solution.py:127
  58.4 2.2 fusion.57
  60.7 1.1 fusion.48
  61.8 0.0 all-gather.19.cloned.1.call-update
  61.8 0.7 all-gather.17.cloned.1.call-done
  62.5 2.1 fusion.61
  64.6 0.0 copy-start.1
  64.6 16.0 %all-gather.15.cloned.1.call-done = bf16[256,2304]{0,1:T(8,128)(2,1)} async-done(((bf16[256,576]{0,1:T(8,128)(2,1)}), bf16[256,2304]{0,1:T(8,128)(2,1)}) %all-gather.15.cloned.1.call-update) | async-done | bytes 1179664 | tf_op jit(solution)/shard_map/all_gather | solution.py:128
  80.6 2.1 fusion.59
  82.7 0.4 select_reduce_fusion
  83.0 0.3 fusion.51
  83.3 0.2 fusion.18
  83.5 20.4 %all-gather.10 = f32[16,1,256]{2,1,0:T(1,128)S(1)} all-gather(f32[1,1,256]{2,1,0:T(1,128)S(1)} %bitcast.189), channel_id=9, replica_groups=mesh['grp'=2,'sv'=4,'tv'=4] {'sv','tv'}, dimensions={0}, use_global_device_ids=true | all-gather | bytes 17408 | tf_op jit(solution)/shard_map/all_gather | solution.py:11
  103.9 17.5 %all-gather.5 = f32[4096,2]{0,1:T(2,128)S(1)} all-gather(f32[256,2]{0,1:T(2,128)S(1)} %get-tuple-element.459), channel_id=7, replica_groups=mesh['grp'=2,'sv'=4,'tv'=4] {'sv','tv'}, dimensions={0}, use_global_device_ids=true | all-gather | bytes 34816 | tf_op jit(solution)/shard_map/all_gather | solution.py:11
  121.4 18.9 %all-gather.6 = f32[4096,2]{0,1:T(2,128)S(1)} all-gather(f32[256,2]{0,1:T(2,128)S(1)} %get-tuple-element.506), channel_id=8, replica_groups=mesh['grp'=2,'sv'=4,'tv'=4] {'sv','tv'}, dimensions={0}, use_global_device_ids=true | all-gather | bytes 34816 | tf_op jit(solution)/shard_map/all_gather | solution.py:11
  140.3 17.5 %all-gather.8 = f32[4096,2]{0,1:T(2,128)S(1)} all-gather(f32[256,2]{0,1:T(2,128)S(1)} %get-tuple-element.458), channel_id=10, replica_groups=mesh['grp'=2,'sv'=4,'tv'=4] {'sv','tv'}, dimensions={0}, use_global_device_ids=true | all-gather | bytes 34816 | tf_op jit(solution)/shard_map/all_gather | solution.py:11
  157.8 1.5 while.43
  159.3 0.6 slice.103
  159.9 0.6 slice.106
  160.5 0.6 fusion.53
  161.0 3.0 %reshape.67 = f32[4,256,448]{1,0,2:T(4,128)} reshape(f32[1024,448]{0,1:T(8,128)} %all-gather.19.cloned.1.call-done) | data formatting | bytes 3670016 | tf_op jit(solution)/shard_map/all_gather | solution.py:133
  164.0 2.6 reduce_sum.83
  166.6 19.8 %all_gather.69 = bf16[256,1792]{0,1:T(8,128)(2,1)S(1)} all-gather(bf16[256,448]{0,1:T(8,128)(2,1)S(1)} %reduce_sum.83), channel_id=1, replica_groups=mesh['grp'=2,'sv'=4,'tv'=4] {'sv'}, dimensions={1}, use_global_device_ids=true | all-gather | bytes 1146880 | tf_op jit(solution)/shard_map/all_gather | solution.py:136
  186.4 2.1 fusion.58
  188.6 0.4 select_reduce_fusion.1
  189.0 0.3 fusion.52
  189.3 0.2 fusion.20
  189.4 19.7 %all-gather.9 = f32[16,1,256]{2,1,0:T(1,128)S(1)} all-gather(f32[1,1,256]{2,1,0:T(1,128)S(1)} %bitcast.190), channel_id=5, replica_groups=mesh['grp'=2,'sv'=4,'tv'=4] {'sv','tv'}, dimensions={0}, use_global_device_ids=true | all-gather | bytes 17408 | tf_op jit(solution)/shard_map/all_gather | solution.py:11
  209.1 17.5 %all-gather.1 = f32[4096,2]{0,1:T(2,128)S(1)} all-gather(f32[256,2]{0,1:T(2,128)S(1)} %get-tuple-element.461), channel_id=3, replica_groups=mesh['grp'=2,'sv'=4,'tv'=4] {'sv','tv'}, dimensions={0}, use_global_device_ids=true | all-gather | bytes 34816 | tf_op jit(solution)/shard_map/all_gather | solution.py:11
  226.6 18.9 %all-gather.2 = f32[4096,2]{0,1:T(2,128)S(1)} all-gather(f32[256,2]{0,1:T(2,128)S(1)} %get-tuple-element.508), channel_id=4, replica_groups=mesh['grp'=2,'sv'=4,'tv'=4] {'sv','tv'}, dimensions={0}, use_global_device_ids=true | all-gather | bytes 34816 | tf_op jit(solution)/shard_map/all_gather | solution.py:11
  245.4 17.5 %all-gather.4 = f32[4096,2]{0,1:T(2,128)S(1)} all-gather(f32[256,2]{0,1:T(2,128)S(1)} %get-tuple-element.460), channel_id=6, replica_groups=mesh['grp'=2,'sv'=4,'tv'=4] {'sv','tv'}, dimensions={0}, use_global_device_ids=true | all-gather | bytes 34816 | tf_op jit(solution)/shard_map/all_gather | solution.py:11
  262.9 1.6 while.42
  264.5 0.0 copy-start.7
  264.5 1.5 subtract_exponential_fusion.2
  266.1 0.0 copy-start.9
  266.1 0.0 copy-start.10
  266.1 0.0 copy-start.11
  266.2 1.1 fusion.11
  267.3 0.0 copy-done.8
  267.3 0.6 fusion.37
  (187 shorter events, 1.9 us)
Async XLA Ops:
  8.0 54.5 %copy-start = (bf16[2304,512]{1,0:T(8,128)(2,1)S(1)}, bf16[2304,512]{1,0:T(8,128)(2,1)}, u32[]{:S(2)}) copy-start(bf16[2304,512]{1,0:T(8,128)(2,1)} %param.27) | copy-start | bytes 7077892
  8.0 38.1 %copy-start.15 = (s32[2]{0:T(128)S(1)}, s32[2]{0:T(128)}, u32[]{:S(2)}) copy-start(s32[2]{0:T(128)} %param.23) | copy-start | bytes 28
  8.0 38.1 %all-reduce.3.cloned.1.call-start = ((), (), s32[]{:S(2)}) async-start(), calls=%async_computation | async-start | bytes 262144 | tf_op jit(solution)/shard_map/psum | solution.py:27
  9.9 52.6 %all-gather.17.cloned.1.call-start = ((), (), s32[]{:S(2)}) async-start(), calls=%async_computation.2 | async-start | bytes 1474560 | tf_op jit(solution)/shard_map/all_gather | solution.py:135
  11.5 38.3 %copy-start.14 = (s32[2]{0:T(128)S(1)}, s32[2]{0:T(128)}, u32[]{:S(2)}) copy-start(s32[2]{0:T(128)} %param.22) | copy-start | bytes 28
  11.5 38.4 %copy-start.12 = (s32[256]{0:T(256)S(1)}, s32[256]{0:T(256)}, u32[]{:S(2)}) copy-start(s32[256]{0:T(256)} %param.20) | copy-start | bytes 3076
  11.5 38.4 %copy-start.13 = (s32[256]{0:T(256)S(1)}, s32[256]{0:T(256)}, u32[]{:S(2)}) copy-start(s32[256]{0:T(256)} %param.21) | copy-start | bytes 3076
  11.6 39.0 %copy-start.3 = (bf16[256,448]{0,1:T(8,128)(2,1)S(1)}, bf16[256,448]{0,1:T(8,128)(2,1)}, u32[]{:S(2)}) copy-start(bf16[256,448]{0,1:T(8,128)(2,1)} %param.16) | copy-start | bytes 688132
  31.4 49.2 %all-gather.15.cloned.1.call-start = ((), (), s32[]{:S(2)}) async-start(), calls=%async_computation.1 | async-start | bytes 1474560 | tf_op jit(solution)/shard_map/all_gather | solution.py:128
  49.8 111.3 %all-gather.19.cloned.1.call-start = ((), (), s32[]{:S(2)}) async-start(), calls=%async_computation.3 | async-start | bytes 2293760 | tf_op jit(solution)/shard_map/all_gather | solution.py:133
  49.9 10.7 %copy-start.5 = (s32[256]{0:T(256)}, s32[256]{0:T(256)S(1)}, u32[]{:S(2)}) copy-start(s32[256]{0:T(256)S(1)} %fusion.35) | copy-start | bytes 3076
  58.4 2.2 copy-start.4
  64.6 18.7 %copy-start.1 = (f32[256,512]{1,0:T(8,128)}, f32[256,512]{1,0:T(8,128)S(1)}, u32[]{:S(2)}) copy-start(f32[256,512]{1,0:T(8,128)S(1)} %fusion.61) | copy-start | bytes 1572868
  82.6 0.8 copy-start.2
  264.5 1.7 copy-start.7
  266.1 1.2 copy-start.6
  266.1 1.2 copy-start.8
  266.1 1.2 copy-start.9
  266.1 1.2 copy-start.10
  266.1 1.2 copy-start.11
Sparse Core Ops, SparseCore 0:
  11.7 34.3 all-reduce.2
Sparse Core Ops, SparseCore 1:
  31.5 31.0 all-gather.16
  64.0 16.5 all-gather.14
  82.1 21.0 all-gather.18
